TPU v7x, 512 devices: a whole 4x8x8 slice. The times are simulated.
512 devices in a mesh: gx: 4 (over x), gy: 16 (over z, core), gz: 8 (over y).
Axes of the slice: x: 4, y: 8, z: 8, core: 2. Of those that a mesh axis runs over, the one named last changes fastest.
Arguments:
- sketch: float32 [8, 32, 16, 64, 384], P('gx', 'gy', 'gz'), may hold values from -1200 to 1200
- test_matrix: bfloat16 [8, 32, 16, 64, 384], P('gx', 'gy', 'gz'), may hold values from -0.1796875 to 0.1796875
- offsets: bfloat16 [8, 32, 16, 3, 128], P('gx', 'gy', 'gz'), may hold values from 0 to 1
- near: int32 [8, 32, 16, 27], P('gx', 'gy', 'gz'), may hold values 0 or 1
Outputs:
- leaf_basis: float32 [8, 32, 16, 64, 384], P('gx', 'gy', 'gz')
- level1_transfer: float32 [4, 16, 8, 64, 512], P('gx', 'gy', 'gz')
- level2_basis: float32 [8, 32, 16, 64, 384], P('gx', 'gy', 'gz')
All inputs are finite; a program needn't handle non-finite values. No bound on the sum of `near` on one device may be relied on, other than what follows from the above.
Results may differ from a plain program's by a relative error of at most 0.0029.
Values may be sent and summed in bfloat16 or wider, within the bound.
A program may use at most 64 MiB of HBM per device.

v0:
```python
import math

import jax
import jax.numpy as jnp
from jax import lax
from jax.sharding import PartitionSpec as P

EPSILON = 0.1
HIGHEST = lax.Precision.HIGHEST


def with_halo(x, sides, width):
    for axis, dim in sides:
        size, length = (lax.axis_size(axis), x.shape[dim])
        up = [(i, (i + 1) % size) for i in range(size - 1)]
        down = [(j, i) for i, j in up]
        last = lax.slice_in_dim(x, length - width, length, axis=dim)
        initial = lax.slice_in_dim(x, 0, width, axis=dim)
        before = lax.ppermute(last, axis, up)
        after = lax.ppermute(initial, axis, down)
        x = jnp.concatenate([before, x, after], axis=dim)
    return x


def from_partner(x, axis, distance):
    return lax.ppermute(x, axis, [(i, i ^ 1 << distance) for i in range(lax.axis_size(axis))])


def orthonormal(rows_t):
    gram_matrix = jnp.einsum("...km,...lm->...kl", rows_t, rows_t, precision=HIGHEST)
    first_factor = jnp.linalg.cholesky(gram_matrix)
    orthogonal = lax.linalg.triangular_solve(first_factor, rows_t, left_side=True, lower=True)
    gram_matrix = jnp.einsum("...km,...lm->...kl", orthogonal, orthogonal, precision=HIGHEST)
    second = jnp.linalg.cholesky(gram_matrix)
    orthogonal = lax.linalg.triangular_solve(second, orthogonal, left_side=True, lower=True)
    return (orthogonal, jnp.matmul(first_factor, second, precision=HIGHEST))


def shift_table():
    offset_index = jnp.arange(27, dtype=jnp.int32)
    offset_steps = jnp.stack([offset_index // 9, offset_index // 3 % 3, offset_index % 3], axis=1)
    return (1 - offset_steps).astype(jnp.float32)


def kernel_tiles(own_offsets, near_offsets, shifts):
    separation = (
        shifts[None, :, :, None, None]
        + own_offsets[:, None, :, :, None]
        - near_offsets[:, :, :, None, :]
    )
    square = jnp.sum(separation * separation, axis=2)
    softened = square + EPSILON * EPSILON
    inverse = 1.0 / (softened * jnp.sqrt(softened))
    diagonal = (square + 2.0 * EPSILON * EPSILON) * inverse
    identity = jnp.eye(3, dtype=jnp.float32)
    kernel_block = (
        separation[:, :, :, None] * separation[:, :, None, :] * inverse[:, :, None, None]
        + identity[None, None, :, :, None, None] * diagonal[:, :, None, None]
    )
    return kernel_block.astype(jnp.bfloat16)


def join_sorted(grouped, partner, parity):
    return jnp.where(
        parity == 0,
        jnp.concatenate([grouped, partner], axis=0),
        jnp.concatenate([partner, grouped], axis=0),
    )


def body(sketch, test_matrix, offsets, near):
    leaf_side = sketch.shape[0]
    basis_rank = sketch.shape[3]
    leaf_rows = sketch.shape[4]
    node_count = offsets.shape[4]
    leaf_count = leaf_side * leaf_side * leaf_side
    packed = jnp.concatenate(
        [
            test_matrix.reshape(leaf_side, leaf_side, leaf_side, basis_rank * leaf_rows),
            offsets.reshape(leaf_side, leaf_side, leaf_side, 3 * node_count),
        ],
        axis=3,
    )
    extended = with_halo(packed, (("gx", 0), ("gy", 1), ("gz", 2)), 1)
    packed_width = packed.shape[3]
    sample_width = basis_rank * leaf_rows
    shifts = shift_table()
    flat_sketch = sketch.reshape(leaf_count, basis_rank, leaf_rows)
    flat_offsets = offsets.reshape(leaf_count, 3, node_count).astype(jnp.float32)
    flat_near = near.reshape(leaf_count, 27).astype(jnp.bfloat16)

    def correct(leaf_index):
        corner_x = leaf_index // (leaf_side * leaf_side)
        corner_y = leaf_index // leaf_side % leaf_side
        corner_z = leaf_index % leaf_side
        zero = jnp.zeros((), jnp.int32)
        own_offsets = flat_offsets[leaf_index][None]
        near_mask = flat_near[leaf_index]
        correction = jnp.zeros((basis_rank, 3, node_count), jnp.float32)
        for slab in range(3):
            neighbours = lax.dynamic_slice(
                extended, (corner_x + slab, corner_y, corner_z, zero), (1, 3, 3, packed_width)
            ).reshape(9, packed_width)
            sampled = neighbours[:, :sample_width].reshape(9, basis_rank, 3, node_count)
            sampled = sampled * near_mask[slab * 9 : slab * 9 + 9][:, None, None, None]
            near_offsets = (
                neighbours[:, sample_width:].reshape(9, 3, node_count).astype(jnp.float32)
            )
            kernel_block = kernel_tiles(
                own_offsets, near_offsets[None], shifts[slab * 9 : slab * 9 + 9]
            )[0]
            correction = correction + jnp.einsum(
                "kpqij,kcqj->cpi", kernel_block, sampled, preferred_element_type=jnp.float32
            )
        return flat_sketch[leaf_index] - correction.reshape(basis_rank, leaf_rows)

    far_field = lax.map(correct, jnp.arange(leaf_count, dtype=jnp.int32))
    leaf_t, leaf_lower = orthonormal(far_field)
    stacked = jnp.transpose(leaf_lower, (1, 0, 2)).reshape(basis_rank, leaf_count * basis_rank)
    level_t, level_lower = orthonormal(stacked)
    parity_x = lax.axis_index("gx") % 2
    parity_y = lax.axis_index("gy") % 2
    parity_z = lax.axis_index("gz") % 2
    grouped = level_lower[None]
    partner = from_partner(grouped, "gz", 0)
    grouped = join_sorted(grouped, partner, parity_z)
    partner = from_partner(grouped, "gy", 0)
    grouped = join_sorted(grouped, partner, parity_y)
    partner = from_partner(grouped, "gx", 0)
    grouped = join_sorted(grouped, partner, parity_x)
    merged = jnp.transpose(grouped, (1, 0, 2)).reshape(basis_rank, 8 * basis_rank)
    merged_t, merged_lower = orthonormal(merged)
    position = (parity_x * 2 + parity_y) * 2 + parity_z
    top_block = lax.dynamic_slice_in_dim(merged_t, position * basis_rank, basis_rank, axis=1)
    child_blocks = jnp.transpose(level_t.reshape(basis_rank, leaf_count, basis_rank), (1, 0, 2))
    mixing = jnp.einsum("rk,akl->arl", top_block, child_blocks, precision=HIGHEST)
    nested = jnp.einsum("arl,aln->arn", mixing, leaf_t, precision=HIGHEST) * (
        8.0 * math.sqrt(leaf_rows)
    )
    leaf_out = (leaf_t * math.sqrt(leaf_rows)).reshape(
        leaf_side, leaf_side, leaf_side, basis_rank, leaf_rows
    )
    level_out = (level_t * math.sqrt(8 * basis_rank))[None, None, None]
    return (
        leaf_out,
        level_out,
        nested.reshape(leaf_side, leaf_side, leaf_side, basis_rank, leaf_rows),
    )


def solution(mesh):
    placed = (
        P("gx", "gy", "gz", None, None),
        P("gx", "gy", "gz", None, None),
        P("gx", "gy", "gz", None, None),
        P("gx", "gy", "gz", None),
    )
    return jax.shard_map(
        body,
        mesh=mesh,
        in_specs=placed,
        out_specs=(
            P("gx", "gy", "gz", None, None),
            P("gx", "gy", "gz", None, None),
            P("gx", "gy", "gz", None, None),
        ),
        check_vma=False,
    )
```

profile of v0, /device:TPU:306, one launch (start us, length us, event | category | flops | bytes accessed | tf_op | source)
XLA Modules:
  0.0 516.9 jit_solution(14418968497338351381)
XLA Ops:
  3.4 3.4 collective-permute-start
  6.8 2.5 collective-permute-start.1
  9.3 7.0 %collective-permute-done = bf16[1,2,2,24960]{3,0,2,1:T(2,128)(2,1)S(1)} collective-permute-done((bf16[1,2,2,24960]{3,0,2,1:T(2,128)(2,1)S(1)}, bf16[1,2,2,24960]{3,0,2,1:T(2,128)(2,1)S(1)}, u32[]{:S(2)}, u32[]{:S(2)}) %collective-permute-start) | collective-permute-done | bytes 199712 | tf_op jit(solution)/shard_map/ppermute | solution.py:19
  16.3 3.1 collective-permute-done.1
  19.4 1.3 pad_maximum_fusion.2
  21.0 1.9 collective-permute-start.2
  23.0 4.9 collective-permute-start.3
  27.8 3.6 collective-permute-done.2
  31.4 1.8 collective-permute-done.3
  33.2 1.7 pad_maximum_fusion.1
  35.8 3.3 collective-permute-start.5
  40.3 3.5 collective-permute-start.4
  44.6 13.5 %collective-permute-done.5 = bf16[4,4,1,24960]{3,1,2,0:T(4,128)(2,1)} collective-permute-done((bf16[4,4,1,24960]{3,1,2,0:T(4,128)(2,1)S(1)}, bf16[4,4,1,24960]{3,1,2,0:T(4,128)(2,1)}, u32[]{:S(2)}, u32[]{:S(2)}) %collective-permute-start.5) | collective-permute-done | bytes 798752 | tf_op jit(solution)/shard_map/ppermute | solution.py:20
  58.1 1.4 copy.106
  59.5 2.9 collective-permute-done.4
  62.5 1.4 copy.105
  63.9 2.5 pad_maximum_fusion
  66.4 2.9 copy.108
  69.8 195.8 %while.13 = (s32[]{:T(128)}, f32[8,64,384]{2,1,0:T(8,128)}, s32[8]{0:T(128)}, f32[8,64,384]{2,1,0:T(8,128)}, bf16[4,4,4,24960]{3,2,1,0:T(4,128)(2,1)}, /*index=5...) while((s32[]{:T(128)}, f32[8,64,384]{2,1,0:T(8,128)}, ...), condition=%wide.region_4.5_spmd, body=%wide.region_0.4_spmd.sunk | while | flops 537350464 | bytes 41582560 | solution.py:117
  76.3 2.4 constant_dynamic-slice_fusion.6
  88.2 1.3 fusion.113
  93.1 1.6 subtract_dynamic-update-slice_fusion.2
  100.7 2.4 constant_dynamic-slice_fusion.6
  112.6 1.3 fusion.113
  117.5 1.6 subtract_dynamic-update-slice_fusion.2
  125.1 2.4 constant_dynamic-slice_fusion.6
  137.0 1.3 fusion.113
  141.9 1.6 subtract_dynamic-update-slice_fusion.2
  149.5 2.4 constant_dynamic-slice_fusion.6
  161.4 1.3 fusion.113
  166.3 1.6 subtract_dynamic-update-slice_fusion.2
  173.9 2.4 constant_dynamic-slice_fusion.6
  185.8 1.3 fusion.113
  190.7 1.6 subtract_dynamic-update-slice_fusion.2
  198.3 2.4 constant_dynamic-slice_fusion.6
  210.2 1.3 fusion.113
  215.1 1.6 subtract_dynamic-update-slice_fusion.2
  222.7 2.4 constant_dynamic-slice_fusion.6
  234.6 1.3 fusion.113
  239.5 1.6 subtract_dynamic-update-slice_fusion.2
  247.1 2.4 constant_dynamic-slice_fusion.6
  259.0 1.3 fusion.113
  263.9 1.6 subtract_dynamic-update-slice_fusion.2
  265.6 2.4 fusion.62
  268.2 46.9 %custom-call.16 = f32[8,64,64]{2,1,0:T(8,128)S(1)} custom-call(f32[8,64,64]{2,1,0:T(8,128)S(1)} %fusion.24), custom_call_target="Cholesky" | custom-call | tf_op jit(solution)/shard_map/jit(cholesky)/cholesky | solution.py:31
  315.4 39.3 %custom-call.17 = f32[8,1,64,64]{2,3,1,0:T(8,128)S(1)} custom-call(f32[8,1,64,64]{3,2,1,0:T(8,128)S(1)} %select_bitcast_fusion.1), custom_call_target="InvertDiagBlocksLowerTriangular" | custom-call | tf_op jit(solution)/shard_map/triangular_solve/custom-call.2 | solution.py:32
  354.7 2.0 fusion.22
  357.9 46.9 %custom-call.18 = f32[8,64,64]{2,1,0:T(8,128)S(1)} custom-call(f32[8,64,64]{2,1,0:T(8,128)S(1)} %fusion.21), custom_call_target="Cholesky" | custom-call | tf_op jit(solution)/shard_map/jit(cholesky)/cholesky | solution.py:34
  406.1 39.3 %custom-call.19 = f32[8,1,64,64]{2,3,1,0:T(8,128)S(1)} custom-call(f32[8,1,64,64]{3,2,1,0:T(8,128)S(1)} %select_bitcast_fusion), custom_call_target="InvertDiagBlocksLowerTriangular" | custom-call | tf_op jit(solution)/shard_map/triangular_solve/custom-call.2 | solution.py:35
  445.7 5.8 %cholesky.139 = f32[64,64]{1,0:T(8,128)S(1)} custom-call(f32[64,64]{1,0:T(8,128)S(1)} %fusion.45), custom_call_target="Cholesky" | custom-call | tf_op jit(solution)/shard_map/jit(cholesky)/cholesky | solution.py:31
  452.8 4.9 custom-call.20
  458.4 5.8 %cholesky.150 = f32[64,64]{1,0:T(8,128)S(1)} custom-call(f32[64,64]{1,0:T(8,128)S(1)} %fusion.42), custom_call_target="Cholesky" | custom-call | tf_op jit(solution)/shard_map/jit(cholesky)/cholesky | solution.py:34
  465.0 1.5 convolution_bitcast_fusion.1
  466.4 3.7 collective-permute-start.6
  470.1 1.7 broadcast_multiply_fusion.3
  472.5 4.9 custom-call.21
  477.5 1.9 collective-permute-start.7
  480.6 2.5 collective-permute-start.8
  483.9 4.2 collective-permute-done.8
  488.8 5.8 %cholesky.161 = f32[64,64]{1,0:T(8,128)S(1)} custom-call(f32[64,64]{1,0:T(8,128)S(1)} %fusion.39), custom_call_target="Cholesky" | custom-call | tf_op jit(solution)/shard_map/jit(cholesky)/cholesky | solution.py:31
  496.0 4.9 custom-call.22
  501.6 5.8 %cholesky.172 = f32[64,64]{1,0:T(8,128)S(1)} custom-call(f32[64,64]{1,0:T(8,128)S(1)} %fusion.36), custom_call_target="Cholesky" | custom-call | tf_op jit(solution)/shard_map/jit(cholesky)/cholesky | solution.py:34
  508.8 4.9 custom-call.23
  515.0 1.7 convolution_multiply_fusion
  (386 shorter events, 140.0 us)
Async XLA Ops:
  3.4 12.9 %collective-permute-start = (bf16[1,2,2,24960]{3,0,2,1:T(2,128)(2,1)S(1)}, bf16[1,2,2,24960]{3,0,2,1:T(2,128)(2,1)S(1)}, u32[]{:S(2)}, u32[]{:S(2)}) collective-permute-start(bf16[1,2,2,24960]{3,0,2,1:T(2,128)(2,1)S(1)} %get-tuple-element.217), channel_id=1, source_target_pairs={{0,128},{128,256},{256,384},{1,129},{129,257},{257,385},{2,130},{1... | collective-permute-start | bytes 599048 | tf_op jit(solution)/shard_map/ppermute | solution.py:19
  6.8 12.6 %collective-permute-start.1 = (bf16[1,2,2,24960]{3,0,2,1:T(2,128)(2,1)S(1)}, bf16[1,2,2,24960]{3,0,2,1:T(2,128)(2,1)S(1)}, u32[]{:S(2)}, u32[]{:S(2)}) collective-permute-start(bf16[1,2,2,24960]{3,0,2,1:T(2,128)(2,1)S(1)} %get-tuple-element.218), channel_id=1, source_target_pairs={{128,0},{256,128},{384,256},{129,1},{257,129},{385,257},{130,2},{2... | collective-permute-start | bytes 599048 | tf_op jit(solution)/shard_map/ppermute | solution.py:20
  21.0 10.4 %collective-permute-start.2 = (bf16[4,1,2,24960]{3,0,2,1:T(4,128)(2,1)S(1)}, bf16[4,1,2,24960]{3,0,2,1:T(4,128)(2,1)S(1)}, u32[]{:S(2)}, u32[]{:S(2)}) collective-permute-start(bf16[4,1,2,24960]{3,0,2,1:T(4,128)(2,1)S(1)} %get-tuple-element.215), channel_id=1, source_target_pairs={{0,8},{8,16},{16,24},{24,32},{32,40},{40,48},{48,56},{56,64},{64,7... | collective-permute-start | bytes 1198088 | tf_op jit(solution)/shard_map/ppermute | solution.py:19
  23.0 10.2 %collective-permute-start.3 = (bf16[4,1,2,24960]{3,0,2,1:T(4,128)(2,1)S(1)}, bf16[4,1,2,24960]{3,0,2,1:T(4,128)(2,1)S(1)}, u32[]{:S(2)}, u32[]{:S(2)}) collective-permute-start(bf16[4,1,2,24960]{3,0,2,1:T(4,128)(2,1)S(1)} %get-tuple-element.216), channel_id=1, source_target_pairs={{8,0},{16,8},{24,16},{32,24},{40,32},{48,40},{56,48},{64,56},{72,6... | collective-permute-start | bytes 1198088 | tf_op jit(solution)/shard_map/ppermute | solution.py:20
  34.9 8.9 %copy-start.2 = (bf16[2,2,2,3,128]{4,2,3,1,0:T(2,128)(2,1)S(1)}, bf16[2,2,2,3,128]{4,2,3,1,0:T(2,128)(2,1)}, u32[]{:S(2)}) copy-start(bf16[2,2,2,3,128]{4,2,3,1,0:T(2,128)(2,1)} %param.14) | copy-start | bytes 18436
  34.9 8.9 %copy-start.3 = (s32[2,2,2,27]{3,2,1,0:T(2,128)S(1)}, s32[2,2,2,27]{3,2,1,0:T(2,128)}, u32[]{:S(2)}) copy-start(s32[2,2,2,27]{3,2,1,0:T(2,128)} %param.15) | copy-start | bytes 2596
  35.8 22.2 %collective-permute-start.5 = (bf16[4,4,1,24960]{3,1,2,0:T(4,128)(2,1)S(1)}, bf16[4,4,1,24960]{3,1,2,0:T(4,128)(2,1)}, u32[]{:S(2)}, u32[]{:S(2)}) collective-permute-start(bf16[4,4,1,24960]{3,1,2,0:T(4,128)(2,1)S(1)} %copy.104), channel_id=1, source_target_pairs={{1,0},{2,1},{3,2},{4,3},{5,4},{6,5},{7,6},{9,8},{10,9},{11,10},{12... | collective-permute-start | bytes 2396168 | tf_op jit(solution)/shard_map/ppermute | solution.py:20
  40.3 22.2 %collective-permute-start.4 = (bf16[4,4,1,24960]{3,1,2,0:T(4,128)(2,1)}, bf16[4,4,1,24960]{3,1,2,0:T(4,128)(2,1)}, u32[]{:S(2)}, u32[]{:S(2)}) collective-permute-start(bf16[4,4,1,24960]{3,1,2,0:T(4,128)(2,1)} %copy.103), channel_id=1, source_target_pairs={{0,1},{1,2},{2,3},{3,4},{4,5},{5,6},{6,7},{8,9},{9,10},{10,11},{11... | collective-permute-start | bytes 2396168 | tf_op jit(solution)/shard_map/ppermute | solution.py:19
  85.9 2.3 copy-start
  86.0 2.3 copy-start.1
  110.3 2.3 copy-start
  110.3 2.3 copy-start.1
  134.7 2.3 copy-start
  134.7 2.3 copy-start.1
  159.1 2.3 copy-start
  159.1 2.3 copy-start.1
  183.5 2.3 copy-start
  183.5 2.3 copy-start.1
  207.9 2.3 copy-start
  207.9 2.3 copy-start.1
  232.3 2.3 copy-start
  232.3 2.3 copy-start.1
  256.7 2.3 copy-start
  256.7 2.3 copy-start.1
  466.4 11.0 %collective-permute-start.6 = (f32[1,64,64]{2,1,0:T(8,128)S(1)}, f32[1,64,64]{2,1,0:T(8,128)S(1)}, u32[]{:S(2)}, u32[]{:S(2)}) collective-permute-start(f32[1,64,64]{2,1,0:T(8,128)S(1)} %convolution_bitcast_fusion.1), channel_id=1, source_target_pairs={{0,1},{1,0},{2,3},{3,2},{4,5},{5,4},{6,7},{7,6},{8,9},{9,8},{10,11... | collective-permute-start | bytes 49160 | tf_op jit(solution)/shard_map/ppermute | solution.py:26
  477.5 3.1 collective-permute-start.7
  480.6 7.5 %collective-permute-start.8 = (f32[4,64,64]{2,1,0:T(8,128)S(1)}, f32[4,64,64]{2,1,0:T(8,128)S(1)}, u32[]{:S(2)}, u32[]{:S(2)}) collective-permute-start(f32[4,64,64]{2,1,0:T(8,128)S(1)} %maximum_select_fusion.1), channel_id=1, source_target_pairs={{0,128},{128,0},{256,384},{384,256},{1,129},{129,1},{257,385},{385... | collective-permute-start | bytes 196616 | tf_op jit(solution)/shard_map/ppermute | solution.py:26
where the time goes:
time: 525 us; the launch traced here: 517 us
  other arithmetic  294 us (56%)
  local copies, waits for them, and re-layouts  78.9 us (15%)
  matrix products  44.5 us (8%)
  waiting for transfers between devices  37 us (7%)
  loops' own time  34 us (6%)
  starting transfers between devices  27.4 us (5%)
    another operation x10, other arithmetic, orthonormal(): second = jnp.linalg.cholesky(gram_matrix)  60.1 us
    another operation x9, other arithmetic, orthonormal(): first_factor = jnp.linalg.cholesky(gram_matrix)  60.1 us
    another operation x7, other arithmetic, orthonormal(): lax.linalg.triangular_solve(second, orthogonal, left_side=True, lower=True)  50.5 us
    another operation x6, other arithmetic, orthonormal(): lax.linalg.triangular_solve(first_factor, rows_t, left_side=True, lower=T...  50.5 us
    another operation x1, loops' own time, body(): far_field = lax.map(correct, jnp.arange(leaf_count, dtype=jnp.int32))  34 us
    dot_general x24, matrix products, correct(): jnp.einsum('kpqij,kcqj->cpi', kernel_block, sampled, preferred_element_ty...  30.3 us
    reshape x24, local copies, waits for them, and re-layouts, correct(): sampled = neighbours[:, :sample_width].reshape(9, basis_rank, 3, node_count)  19.3 us
    dynamic_slice x8, local copies, waits for them, and re-layouts, correct(): lax.dynamic_slice(extended, (corner_x + slab, corner_y, corner_z, zero),...  19 us
  transfers between devices with their start and end apart: 9, of which 8 were waited for; matrix products, arithmetic and copies ran while one was open for 2% of the time, Pallas kernels for 0%

commit v1 on v0

v1 whole, which is shorter than its diff:
```python
import functools
import math

import jax
import jax.numpy as jnp
from jax import lax
from jax.experimental import pallas as pl
from jax.experimental.pallas import tpu as pltpu
from jax.sharding import PartitionSpec as P

EPS2 = 0.1 * 0.1
HIGHEST = lax.Precision.HIGHEST
MESH = pl.DeviceIdType.MESH
NODES = 128
F32 = jnp.float32
BF16 = jnp.bfloat16
UNROLL = 8
RANK = 64
BLOCK = 8


def directions():
    out = []
    for dx in (-1, 0, 1):
        for dy in (-1, 0, 1):
            for dz in (-1, 0, 1):
                if (dx, dy, dz) != (0, 0, 0):
                    out.append((dx, dy, dz))
    return out


def source_window(d):
    return [pl.ds(0, 2) if s == 0 else pl.ds((s + 1) // 2, 1) for s in d]


def landing_window(d):
    return [pl.ds(1, 2) if s == 0 else pl.ds(0 if s == 1 else 3, 1) for s in d]


def tile(a_rows, spread, out):
    for j in range(0, NODES, 16):
        r = [a_rows[p] - spread[p, j : j + 16, :] for p in range(3)]
        square = r[0] * r[0] + r[1] * r[1] + r[2] * r[2]
        root = lax.rsqrt(square + EPS2)
        h = root * root * root
        diagonal = (square + 2.0 * EPS2) * h
        scaled = [r[p] * h for p in range(3)]
        for p in range(3):
            for q in range(p, 3):
                block = scaled[p] * r[q]
                if p == q:
                    block = block + diagonal
                block = block.astype(BF16)
                out[q * NODES + j : q * NODES + j + 16, p * NODES : (p + 1) * NODES] = block
                if p != q:
                    out[p * NODES + j : p * NODES + j + 16, q * NODES : (q + 1) * NODES] = block


def place(kind, c, leaf, t):
    bits = [leaf // 4, leaf // 2 % 2, leaf % 2]
    first, third = (2 - c) // 2, c // 2
    marks = [first, 1 - first - third, third]
    if kind == 0:
        return [bit + 1 for bit in bits], [t // 4, t // 2 % 2, t % 2]
    if kind == 1:
        high, low = t // 2, t % 2
        b = [m * 3 * bit + (1 - m) * (bit + 1) for m, bit in zip(marks, bits)]
        a = [
            marks[0] * bits[0] + (1 - marks[0]) * high,
            marks[1] * bits[1] + marks[0] * high + marks[2] * low,
            marks[2] * bits[2] + (1 - marks[2]) * low,
        ]
        return b, a
    if kind == 2:
        b = [(1 - m) * 3 * bit + m * (bit + 1) for m, bit in zip(marks, bits)]
        a = [m * t + (1 - m) * bit for m, bit in zip(marks, bits)]
        return b, a
    return [3 * bit for bit in bits], bits


def pair_class(kind, c, near_ref, ext, ext_off, acc, spreads, tiles):
    count = 8 // 2**kind
    per = min(count, UNROLL)
    pick = (
        lax.broadcasted_iota(jnp.int32, (3, 3 * NODES), 1) // NODES
        == lax.broadcasted_iota(jnp.int32, (3, 3 * NODES), 0)
    ).astype(BF16)

    def step(n, carry):
        u = 0
        for m in range(UNROLL // per):
            first = n * UNROLL + m * per
            leaf = first // count
            b, _ = place(kind, c, leaf, 0)
            spread = lax.dot_general(
                ext_off[b[0], b[1], b[2]],
                pick,
                (((0,), (0,)), ((), ())),
                preferred_element_type=F32,
            )
            for p in range(3):
                spreads[m, p] = spread[:, p * NODES : (p + 1) * NODES]
            for k in range(per):
                b, a = place(kind, c, leaf, first % count + k)
                d = [b[k] - 1 - a[k] for k in range(3)]
                own = ext_off[a[0] + 1, a[1] + 1, a[2] + 1].astype(F32)
                rows = [own[p : p + 1, :] - d[p].astype(F32) for p in range(3)]
                tile(rows, spreads.at[m], tiles.at[u])
                index = 9 * (d[0] + 1) + 3 * (d[1] + 1) + d[2] + 1
                mask = near_ref[a[0], a[1], a[2], index].astype(F32)
                sampled = ext[b[0], b[1], b[2]] * mask.astype(BF16)
                acc[a[0], a[1], a[2]] -= jnp.dot(
                    sampled, tiles[u], preferred_element_type=F32
                )
                u += 1
        return carry

    lax.fori_loop(0, 8 * count // UNROLL, step, 0)


def all_pairs(arrive, *refs):
    arrive(0, 0)
    pair_class(0, 0, *refs)
    for kind in (1, 2):

        def step(c, carry):
            arrive(kind, c)
            pair_class(kind, c, *refs)
            return carry

        lax.fori_loop(0, 3, step, 0)
    arrive(3, 0)
    pair_class(3, 0, *refs)


def kind_of(d):
    size = sum(abs(s) for s in d)
    if size == 3:
        return 3, 0
    return size, [abs(s) for s in d].index(1 if size == 1 else 0)


def near_kernel(
    sizes, near_ref, sketch, test, offs, far, ext, ext_off, spreads, tiles, sends, recvs, o_sends, o_recvs
):
    names = ("gx", "gy", "gz")
    me = [lax.axis_index(n) for n in names]

    def inside(d):
        ok = None
        for k in range(3):
            if d[k] != 0:
                here = (me[k] < sizes[k] - 1) if d[k] == 1 else (me[k] > 0)
                ok = here if ok is None else jnp.logical_and(ok, here)
        return ok

    def copies(d):
        n = directions().index(d)
        to = tuple(me[k] + d[k] for k in range(3))
        s, t = source_window(d), landing_window(d)
        return (
            pltpu.make_async_remote_copy(
                src_ref=offs.at[s[0], s[1], s[2]],
                dst_ref=ext_off.at[t[0], t[1], t[2]],
                send_sem=o_sends.at[n],
                recv_sem=o_recvs.at[n],
                device_id=to,
                device_id_type=MESH,
            ),
            pltpu.make_async_remote_copy(
                src_ref=test.at[s[0], s[1], s[2]],
                dst_ref=ext.at[t[0], t[1], t[2]],
                send_sem=sends.at[n],
                recv_sem=recvs.at[n],
                device_id=to,
                device_id_type=MESH,
            ),
        )

    barrier = pltpu.get_barrier_semaphore()
    for d in directions():

        @pl.when(inside(d))
        def _():
            to = tuple(me[k] + d[k] for k in range(3))
            pl.semaphore_signal(barrier, inc=1, device_id=to, device_id_type=MESH)

    spans = [
        1 + (me[k] > 0).astype(jnp.int32) + (me[k] < sizes[k] - 1).astype(jnp.int32)
        for k in range(3)
    ]
    for k in range(3):
        for side in (0, 1):
            at = [slice(None)] * 3
            at[k] = slice(3 * side, 3 * side + 1)

            @pl.when(me[k] == side * (sizes[k] - 1))
            def _():
                ext[at[0], at[1], at[2]] = jnp.zeros_like(ext[at[0], at[1], at[2]])
                ext_off[at[0], at[1], at[2]] = jnp.zeros_like(ext_off[at[0], at[1], at[2]])

    pl.semaphore_wait(barrier, spans[0] * spans[1] * spans[2] - 1)
    order = sorted(directions(), key=kind_of)
    for d in order:

        @pl.when(inside(d))
        def _():
            for c in copies(d):
                c.start()

    ext[1:3, 1:3, 1:3] = test[...]
    ext_off[1:3, 1:3, 1:3] = offs[...]
    far[...] = sketch[...]

    def arrive(kind, c):
        for d in order:
            if kind_of(d)[0] == kind:

                @pl.when(jnp.logical_and(c == kind_of(d)[1], inside([-s for s in d])))
                def _():
                    for copy in copies(d):
                        copy.wait_recv()

    all_pairs(arrive, near_ref, ext, ext_off, far, spreads, tiles)
    for d in order:

        @pl.when(inside(d))
        def _():
            for c in copies(d):
                c.wait_send()


def near_field(mesh, sketch, test, offs, near):
    sizes = tuple(mesh.shape[n] for n in ("gx", "gy", "gz"))
    vmem = pl.BlockSpec(memory_space=pltpu.VMEM)
    return pl.pallas_call(
        functools.partial(near_kernel, sizes),
        out_shape=jax.ShapeDtypeStruct(sketch.shape, F32),
        in_specs=[pl.BlockSpec(memory_space=pltpu.SMEM), vmem, vmem, vmem],
        out_specs=vmem,
        scratch_shapes=[
            pltpu.VMEM((4, 4, 4) + test.shape[3:], BF16),
            pltpu.VMEM((4, 4, 4) + offs.shape[3:], BF16),
            pltpu.VMEM((UNROLL, 3, NODES, NODES), F32),
            pltpu.VMEM((UNROLL, 3 * NODES, 3 * NODES), BF16),
            pltpu.SemaphoreType.DMA((26,)),
            pltpu.SemaphoreType.DMA((26,)),
            pltpu.SemaphoreType.DMA((26,)),
            pltpu.SemaphoreType.DMA((26,)),
        ],
        compiler_params=pltpu.CompilerParams(
            collective_id=0, has_side_effects=True, vmem_limit_bytes=48 << 20
        ),
    )(near, sketch, test, offs)


def gram(rows, stage):
    stage[RANK:, :] = rows
    return lax.dot_general(
        rows,
        stage[...],
        (((1,), (1,)), ((), ())),
        precision=HIGHEST,
        preferred_element_type=F32,
    )


def product(left, right):
    return jnp.dot(left, right, precision=HIGHEST, preferred_element_type=F32)


def put(state, slot, matrix):
    eye = (
        lax.broadcasted_iota(jnp.int32, (RANK, 2 * RANK), 0)
        == lax.broadcasted_iota(jnp.int32, (RANK, 2 * RANK), 1)
    ).astype(F32)
    state[pl.ds(slot, RANK, stride=8), :] = matrix + eye


def inverse_of(state, slot):
    return state[pl.ds(slot, RANK, stride=8), :][:, :RANK]


def splat(row, lane):
    return jnp.broadcast_to(row[:, RANK + lane : RANK + lane + 1], row.shape)


def factor(states):
    for start in range(0, RANK, BLOCK):
        for state in states:
            rows = [state[8 * (start + k) : 8 * (start + k) + 8, :] for k in range(BLOCK)]
            c = {
                (k, m): splat(rows[k], start + m)
                for k in range(BLOCK)
                for m in range(k, BLOCK)
            }
            for k in range(BLOCK):
                inverse = lax.rsqrt(c[k, k])
                f = {m: c[k, m] * inverse for m in range(k + 1, BLOCK)}
                for m in range(k + 1, BLOCK):
                    for n in range(m, BLOCK):
                        c[m, n] = c[m, n] - f[m] * f[n]
                rows[k] = rows[k] * inverse
                for m in range(k + 1, BLOCK):
                    rows[m] = rows[m] - f[m] * rows[k]
                state[8 * (start + k) : 8 * (start + k) + 8, :] = rows[k]
            for i in range(start + BLOCK, RANK):
                row = state[8 * i : 8 * i + 8, :]
                for k in range(BLOCK):
                    row = row - splat(rows[k], i) * rows[k]
                state[8 * i : 8 * i + 8, :] = row


def leaves():
    return [(i, j, k) for i in range(2) for j in range(2) for k in range(2)]


def gram_kernel(far, grams, box, stage):
    stage[:RANK, :] = jnp.zeros((RANK, stage.shape[1]), F32)
    total = None
    for n, a in enumerate(leaves()):
        g = gram(far[a], stage)
        grams[n] = g
        total = g if total is None else total + g
    box[...] = total


def first_kernel(far, grams, box, group, q1, w, v, grams2, box2, group2, leaf_state, top_state, stage):
    stage[:RANK, :] = jnp.zeros((RANK, stage.shape[1]), F32)
    for n in range(8):
        put(leaf_state, n, grams[n])
    put(top_state, 0, box[...])
    for n in range(1, 8):
        put(top_state, n, group[...])
    factor([leaf_state, top_state])
    box_inverse = inverse_of(top_state, 0)
    group_inverse = inverse_of(top_state, 1)
    box_total = group_total = None
    for n, a in enumerate(leaves()):
        rows = far[a]
        x = product(inverse_of(leaf_state, n), rows)
        q1[n] = x
        grams2[n] = gram(x, stage)
        x = product(box_inverse, rows)
        w[n] = x
        g = gram(x, stage)
        box_total = g if box_total is None else box_total + g
        x = product(group_inverse, rows)
        v[n] = x
        g = gram(x, stage)
        group_total = g if group_total is None else group_total + g
    box2[...] = box_total
    group2[...] = group_total


def second_kernel(q1, w, v, grams2, box2, group2, leaf_out, level_out, nested_out, leaf_state, top_state, stage):
    for n in range(8):
        put(leaf_state, n, grams2[n])
    put(top_state, 0, box2[...])
    for n in range(1, 8):
        put(top_state, n, group2[...])
    factor([leaf_state, top_state])
    width = q1.shape[2]
    box_inverse = inverse_of(top_state, 0) * math.sqrt(8 * RANK)
    group_inverse = inverse_of(top_state, 1) * (8.0 * math.sqrt(width))
    for pair in range(4):
        block = None
        for half in range(2):
            n = 2 * pair + half
            a = leaves()[n]
            x = product(inverse_of(leaf_state, n), q1[n])
            leaf_out[a] = x * math.sqrt(width)
            nested_out[a] = product(group_inverse, v[n])
            stage[half * RANK : (half + 1) * RANK, :] = x
            stage[(1 - half) * RANK : (2 - half) * RANK, :] = jnp.zeros((RANK, width), F32)
            part = lax.dot_general(
                product(box_inverse, w[n]),
                stage[...],
                (((1,), (1,)), ((), ())),
                precision=HIGHEST,
                preferred_element_type=F32,
            )
            block = part if block is None else block + part
        level_out[0, 0, 0, :, 2 * RANK * pair : 2 * RANK * (pair + 1)] = block


def exchange_kernel(own, total, slots, sends, recvs):
    names = ("gx", "gy", "gz")
    me = [lax.axis_index(n) for n in names]
    bits = [m % 2 for m in me]
    place = (bits[0] * 2 + bits[1]) * 2 + bits[2]
    others = []
    for n in range(1, 8):
        flip = (n // 4, n // 2 % 2, n % 2)
        others.append(tuple(me[k] + flip[k] * (1 - 2 * bits[k]) for k in range(3)))
    barrier = pltpu.get_barrier_semaphore()
    for to in others:
        pl.semaphore_signal(barrier, inc=1, device_id=to, device_id_type=MESH)
    pl.semaphore_wait(barrier, 7)
    copies = [
        pltpu.make_async_remote_copy(
            src_ref=own,
            dst_ref=slots.at[place],
            send_sem=sends.at[n],
            recv_sem=recvs.at[n],
            device_id=to,
            device_id_type=MESH,
        )
        for n, to in enumerate(others)
    ]
    for c in copies:
        c.start()
    slots[place] = own[...]
    for c in copies:
        c.wait_recv()
    value = slots[0]
    for n in range(1, 8):
        value = value + slots[n]
    total[...] = value
    for c in copies:
        c.wait_send()


VMEM = pl.BlockSpec(memory_space=pltpu.VMEM)


def group_sum(own, number):
    return pl.pallas_call(
        exchange_kernel,
        out_shape=jax.ShapeDtypeStruct(own.shape, F32),
        in_specs=[VMEM],
        out_specs=VMEM,
        scratch_shapes=[
            pltpu.VMEM((8,) + own.shape, F32),
            pltpu.SemaphoreType.DMA((7,)),
            pltpu.SemaphoreType.DMA((7,)),
        ],
        compiler_params=pltpu.CompilerParams(collective_id=number, has_side_effects=True),
    )(own)


def local(kernel, outs, scratch, *args):
    return pl.pallas_call(
        kernel,
        out_shape=[jax.ShapeDtypeStruct(s, F32) for s in outs],
        in_specs=[VMEM] * len(args),
        out_specs=[VMEM] * len(outs),
        scratch_shapes=[pltpu.VMEM(s, F32) for s in scratch],
        compiler_params=pltpu.CompilerParams(vmem_limit_bytes=48 << 20),
    )(*args)


def finish(far, reduce_group):
    width = far.shape[4]
    square, slab = (RANK, 2 * RANK), (8, RANK, width)
    stage, state = (2 * RANK, width), (8 * RANK, 2 * RANK)
    grams, box = local(gram_kernel, [(8,) + square, square], [stage], far)
    group = reduce_group(box, 1)
    q1, w, v, grams2, box2, group2 = local(
        first_kernel,
        [slab, slab, slab, (8,) + square, square, square],
        [state, state, stage],
        far,
        grams,
        box,
        group,
    )
    group2 = reduce_group(group2, 2)
    return local(
        second_kernel,
        [far.shape, (1, 1, 1, RANK, 8 * RANK), far.shape],
        [state, state, stage],
        q1,
        w,
        v,
        grams2,
        box2,
        group2,
    )


def solution(mesh):
    placed = (
        P("gx", "gy", "gz", None, None),
        P("gx", "gy", "gz", None, None),
        P("gx", "gy", "gz", None, None),
        P("gx", "gy", "gz", None),
    )

    def body(sketch, test_matrix, offsets, near):
        far = near_field(mesh, sketch, test_matrix, offsets, near)
        return tuple(finish(far, group_sum))

    return jax.shard_map(
        body,
        mesh=mesh,
        in_specs=placed,
        out_specs=placed[:3],
        check_vma=False,
    )
```

time: 525 us -> 113 us (0.22)
  the two profiles are of different devices: /device:TPU:306 before, /device:TPU:81 now
where the time goes in v1:
time: 113 us
  Pallas kernels  105 us (93%)
  local copies, waits for them, and re-layouts  7.21 us (6%)
    pallas_call x1, Pallas kernels, near_field(): pl.pallas_call(functools.partial(near_kernel, sizes), out_shape=jax.Shape...  46.6 us
    pallas_call x3, Pallas kernels, local(): pl.pallas_call(kernel, out_shape=[jax.ShapeDtypeStruct(s, F32) for s in o...  33.2 us
    pallas_call x2, Pallas kernels, group_sum(): pl.pallas_call(exchange_kernel, out_shape=jax.ShapeDtypeStruct(own.shape,...  24.9 us
    unnamed x21, local copies, waits for them, and re-layouts  7.21 us

profile of v1, /device:TPU:81, one launch (start us, length us, event | category | flops | bytes accessed | tf_op | source)
XLA Modules:
  0.0 112.7 jit_solution(14072007076470449548)
XLA Ops:
  0.6 0.0 copy-start.9
  0.6 0.7 copy.7.offs
  1.3 0.0 copy-done.9
  1.3 0.0 copy-start
  1.4 1.1 %copy-done = f32[2,2,2,64,384]{4,3,2,1,0:T(8,128)S(1)} copy-done((f32[2,2,2,64,384]{4,3,2,1,0:T(8,128)S(1)}, f32[2,2,2,64,384]{4,3,2,1,0:T(8,128)}, u32[]{:S(2)}) %copy-start) | copy-done | bytes 786456
  2.5 0.0 copy-start.1
  2.5 1.0 copy-done.1
  3.5 46.6 %shard_map.67.far = f32[2,2,2,64,384]{4,3,2,1,0:T(8,128)S(1)} custom-call(s32[2,2,2,27]{3,2,1,0:T(2,128)S(1)} %copy-done.9, f32[2,2,2,64,384]{4,3,2,1,0:T(8,128)S(1)} %copy-done, bf16[2,2,2,64,384]{4,3,2,1,0:T(8,128)(2,1)S(1)} %copy-done.1, bf16[2,2,2,3,128]{4,3,2,1,0:T(4,128)(2,1)S(1)} %copy.7.offs), custom_call_target="tpu_custom_call" | custom-call | tf_op jit(solution)/shard_map/pallas_call | solution.py:236
  50.1 2.2 %shard_map.68 = (f32[8,64,128]{2,1,0:T(8,128)S(1)}, f32[64,128]{1,0:T(8,128)S(1)}) custom-call(f32[2,2,2,64,384]{4,3,2,1,0:T(8,128)S(1)} %shard_map.67.far), custom_call_target="tpu_custom_call" | custom-call | tf_op jit(solution)/shard_map/pallas_call | solution.py:443
  52.3 0.0 copy-start.5
  52.3 0.6 copy-done.5
  52.9 0.0 copy-start.6
  52.9 16.4 %shard_map.69.group = f32[64,128]{1,0:T(8,128)} custom-call(f32[64,128]{1,0:T(8,128)} %copy-done.5), custom_call_target="tpu_custom_call" | custom-call | tf_op jit(solution)/shard_map/pallas_call | solution.py:428
  69.3 0.0 copy-done.6
  69.3 0.0 copy-start.7
  69.3 0.7 copy-done.7
  70.0 18.5 %shard_map.70 = (f32[8,64,384]{2,1,0:T(8,128)S(1)}, f32[8,64,384]{2,1,0:T(8,128)S(1)}, f32[8,64,384]{2,1,0:T(8,128)S(1)}, f32[8,64,128]{2,1,0:T(8,128)S(1)}, f32...) custom-call(f32[2,2,2,64,384]{4,3,2,1,0:T(8,128)S(1)} %shard_map.67.far, f32[8,64,128]{2,1,0:T(8,128)S(1)} %get-tuple-element.11.grams, ...), custom_call_target="tpu_custom_call" | custom-call | tf_op jit(solution)/shard_map/pallas_call | solution.py:443
  88.5 0.0 copy-start.2
  88.6 0.7 copy-done.2
  89.3 0.0 copy-start.8
  89.3 0.6 copy-done.8
  89.9 8.6 %shard_map.71.group2 = f32[64,128]{1,0:T(8,128)} custom-call(f32[64,128]{1,0:T(8,128)} %copy-done.8), custom_call_target="tpu_custom_call" | custom-call | tf_op jit(solution)/shard_map/pallas_call | solution.py:428
  98.5 0.0 copy-start.3
  98.5 0.9 copy-done.3
  99.4 0.0 copy-start.4
  99.4 0.8 copy-done.4
  100.2 12.5 %shard_map.72 = (f32[2,2,2,64,384]{4,3,2,1,0:T(8,128)}, f32[1,1,1,64,512]{4,3,2,1,0:T(8,128)}, f32[2,2,2,64,384]{4,3,2,1,0:T(8,128)}) custom-call(f32[8,64,384]{2,1,0:T(8,128)S(1)} %get-tuple-element.13.q1, f32[8,64,384]{2,1,0:T(8,128)S(1)} %get-tuple-element.14.w, f32[8,64,384]{2,1,0:T(8,128)S(1)} %get-tuple-element.15.v, f32[8,64,128]{2,1,0:T(8,128)S(1)} %copy-done.3, ...), custom_call_target="tpu_custom_call" | custom-call | tf_op jit(solution)/shard_map/pallas_call | solution.py:443
Async XLA Ops:
  0.6 0.7 copy-start.9
  1.3 1.1 %copy-start = (f32[2,2,2,64,384]{4,3,2,1,0:T(8,128)S(1)}, f32[2,2,2,64,384]{4,3,2,1,0:T(8,128)}, u32[]{:S(2)}) copy-start(f32[2,2,2,64,384]{4,3,2,1,0:T(8,128)} %sketch.1) | copy-start | bytes 2359300
  2.5 1.0 copy-start.1
  52.3 0.6 copy-start.5
  52.9 16.4 %copy-start.6 = (f32[64,128]{1,0:T(8,128)S(1)}, f32[64,128]{1,0:T(8,128)}, u32[]{:S(2)}) copy-start(f32[64,128]{1,0:T(8,128)} %copy-done.5) | copy-start | bytes 98308
  69.3 0.8 copy-start.7
  88.5 0.7 copy-start.2
  89.3 0.6 copy-start.8
  98.5 1.0 copy-start.3
  99.4 0.8 copy-start.4

commit v2 on v1

--- a/solution.py
+++ b/solution.py
@@ -78,44 +78,45 @@
     return [3 * bit for bit in bits], bits
 
 
-def pair_class(kind, c, near_ref, ext, ext_off, acc, spreads, tiles):
+def pair_class(kind, c, near_ref, ext, ext_off, acc, pick, rows8, spreads, tiles):
     count = 8 // 2**kind
-    per = min(count, UNROLL)
-    pick = (
-        lax.broadcasted_iota(jnp.int32, (3, 3 * NODES), 1) // NODES
-        == lax.broadcasted_iota(jnp.int32, (3, 3 * NODES), 0)
-    ).astype(BF16)
+    for leaf in range(8):
+        b, _ = place(kind, c, leaf, 0)
+        rows8[8 * leaf : 8 * leaf + 3, :] = ext_off[b[0], b[1], b[2]].astype(F32)
+    spread = lax.dot_general(
+        rows8[...].astype(BF16),
+        pick[...],
+        (((0,), (0,)), ((), ())),
+        preferred_element_type=F32,
+    )
+    for n in range(24):
+        spreads[n // 3, n % 3] = spread[:, n * NODES : (n + 1) * NODES]
 
     def step(n, carry):
-        u = 0
-        for m in range(UNROLL // per):
-            first = n * UNROLL + m * per
-            leaf = first // count
-            b, _ = place(kind, c, leaf, 0)
-            spread = lax.dot_general(
-                ext_off[b[0], b[1], b[2]],
-                pick,
-                (((0,), (0,)), ((), ())),
-                preferred_element_type=F32,
+        for u in range(UNROLL):
+            leaf = (n * UNROLL + u) // count
+            b, a = place(kind, c, leaf, (n * UNROLL + u) % count)
+            d = [b[k] - 1 - a[k] for k in range(3)]
+            own = ext_off[a[0] + 1, a[1] + 1, a[2] + 1].astype(F32)
+            rows = [own[p : p + 1, :] - d[p].astype(F32) for p in range(3)]
+            tile(rows, spreads.at[leaf], tiles.at[u])
+            index = 9 * (d[0] + 1) + 3 * (d[1] + 1) + d[2] + 1
+            mask = near_ref[a[0], a[1], a[2], index].astype(F32)
+            sampled = ext[b[0], b[1], b[2]] * mask.astype(BF16)
+            acc[a[0], a[1], a[2]] -= jnp.dot(
+                sampled, tiles[u], preferred_element_type=F32
             )
-            for p in range(3):
-                spreads[m, p] = spread[:, p * NODES : (p + 1) * NODES]
-            for k in range(per):
-                b, a = place(kind, c, leaf, first % count + k)
-                d = [b[k] - 1 - a[k] for k in range(3)]
-                own = ext_off[a[0] + 1, a[1] + 1, a[2] + 1].astype(F32)
-                rows = [own[p : p + 1, :] - d[p].astype(F32) for p in range(3)]
-                tile(rows, spreads.at[m], tiles.at[u])
-                index = 9 * (d[0] + 1) + 3 * (d[1] + 1) + d[2] + 1
-                mask = near_ref[a[0], a[1], a[2], index].astype(F32)
-                sampled = ext[b[0], b[1], b[2]] * mask.astype(BF16)
-                acc[a[0], a[1], a[2]] -= jnp.dot(
-                    sampled, tiles[u], preferred_element_type=F32
-                )
-                u += 1
         return carry
 
     lax.fori_loop(0, 8 * count // UNROLL, step, 0)
+
+
+def prepare(pick, rows8):
+    row = lax.broadcasted_iota(jnp.int32, pick.shape, 0)
+    lane = lax.broadcasted_iota(jnp.int32, pick.shape, 1)
+    wanted = jnp.logical_and(row % 8 < 3, row // 8 * 3 + row % 8 == lane // NODES)
+    pick[...] = wanted.astype(F32).astype(BF16)
+    rows8[...] = jnp.zeros_like(rows8)
 
 
 def all_pairs(arrive, *refs):
@@ -141,7 +142,29 @@
 
 
 def near_kernel(
-    sizes, near_ref, sketch, test, offs, far, ext, ext_off, spreads, tiles, sends, recvs, o_sends, o_recvs
+    sizes,
+    near_ref,
+    sketch,
+    test,
+    offs,
+    far,
+    grams,
+    box,
+    group,
+    ext,
+    ext_off,
+    pick,
+    rows8,
+    spreads,
+    tiles,
+    stage,
+    slots,
+    sends,
+    recvs,
+    o_sends,
+    o_recvs,
+    g_sends,
+    g_recvs,
 ):
     names = ("gx", "gy", "gz")
     me = [lax.axis_index(n) for n in names]
@@ -208,6 +231,7 @@
             for c in copies(d):
                 c.start()
 
+    prepare(pick, rows8)
     ext[1:3, 1:3, 1:3] = test[...]
     ext_off[1:3, 1:3, 1:3] = offs[...]
     far[...] = sketch[...]
@@ -221,7 +245,12 @@
                     for copy in copies(d):
                         copy.wait_recv()
 
-    all_pairs(arrive, near_ref, ext, ext_off, far, spreads, tiles)
+    all_pairs(arrive, near_ref, ext, ext_off, far, pick, rows8, spreads, tiles)
+    leaf_grams(far, grams, box, stage)
+    swaps = group_copies(me, box, slots, g_sends, g_recvs)
+    for c in swaps:
+        c.start()
+    collect(me, swaps, box, slots, group)
     for d in order:
 
         @pl.when(inside(d))
@@ -235,18 +264,27 @@
     vmem = pl.BlockSpec(memory_space=pltpu.VMEM)
     return pl.pallas_call(
         functools.partial(near_kernel, sizes),
-        out_shape=jax.ShapeDtypeStruct(sketch.shape, F32),
+        out_shape=[
+            jax.ShapeDtypeStruct(s, F32)
+            for s in (sketch.shape, (8, RANK, 2 * RANK), (RANK, 2 * RANK), (RANK, 2 * RANK))
+        ],
         in_specs=[pl.BlockSpec(memory_space=pltpu.SMEM), vmem, vmem, vmem],
-        out_specs=vmem,
+        out_specs=[vmem] * 4,
         scratch_shapes=[
             pltpu.VMEM((4, 4, 4) + test.shape[3:], BF16),
             pltpu.VMEM((4, 4, 4) + offs.shape[3:], BF16),
-            pltpu.VMEM((UNROLL, 3, NODES, NODES), F32),
+            pltpu.VMEM((64, 24 * NODES), BF16),
+            pltpu.VMEM((64, NODES), F32),
+            pltpu.VMEM((8, 3, NODES, NODES), F32),
             pltpu.VMEM((UNROLL, 3 * NODES, 3 * NODES), BF16),
+            pltpu.VMEM((2 * RANK, 3 * NODES), F32),
+            pltpu.VMEM((8, RANK, 2 * RANK), F32),
             pltpu.SemaphoreType.DMA((26,)),
             pltpu.SemaphoreType.DMA((26,)),
             pltpu.SemaphoreType.DMA((26,)),
             pltpu.SemaphoreType.DMA((26,)),
+            pltpu.SemaphoreType.DMA((7,)),
+            pltpu.SemaphoreType.DMA((7,)),
         ],
         compiler_params=pltpu.CompilerParams(
             collective_id=0, has_side_effects=True, vmem_limit_bytes=48 << 20
@@ -269,12 +307,25 @@
     return jnp.dot(left, right, precision=HIGHEST, preferred_element_type=F32)
 
 
+def gram_near_identity(rows):
+    high = rows.astype(BF16)
+    low = (rows - high.astype(F32)).astype(BF16)
+    both = jnp.concatenate([high, low], axis=0)
+    parts = lax.dot_general(
+        both, both, (((1,), (1,)), ((), ())), preferred_element_type=F32
+    )
+    half = parts[:RANK] + parts[RANK:]
+    return half + pltpu.roll(half, RANK, axis=1)
+
+
+def with_eye(matrix):
+    row = lax.broadcasted_iota(jnp.int32, (RANK, 2 * RANK), 0)
+    lane = lax.broadcasted_iota(jnp.int32, (RANK, 2 * RANK), 1)
+    return jnp.where(lane < RANK, (row == lane).astype(F32), matrix)
+
+
 def put(state, slot, matrix):
-    eye = (
-        lax.broadcasted_iota(jnp.int32, (RANK, 2 * RANK), 0)
-        == lax.broadcasted_iota(jnp.int32, (RANK, 2 * RANK), 1)
-    ).astype(F32)
-    state[pl.ds(slot, RANK, stride=8), :] = matrix + eye
+    state[pl.ds(slot, RANK, stride=8), :] = with_eye(matrix)
 
 
 def inverse_of(state, slot):
@@ -315,7 +366,7 @@
     return [(i, j, k) for i in range(2) for j in range(2) for k in range(2)]
 
 
-def gram_kernel(far, grams, box, stage):
+def leaf_grams(far, grams, box, stage):
     stage[:RANK, :] = jnp.zeros((RANK, stage.shape[1]), F32)
     total = None
     for n, a in enumerate(leaves()):
@@ -325,32 +376,46 @@
     box[...] = total
 
 
-def first_kernel(far, grams, box, group, q1, w, v, grams2, box2, group2, leaf_state, top_state, stage):
-    stage[:RANK, :] = jnp.zeros((RANK, stage.shape[1]), F32)
+def first_kernel(grams, box, group, leaf_state, top_state):
     for n in range(8):
         put(leaf_state, n, grams[n])
     put(top_state, 0, box[...])
     for n in range(1, 8):
         put(top_state, n, group[...])
     factor([leaf_state, top_state])
+
+
+def apply_kernel(
+    far, leaf_state, top_state, q1, w, v, grams2, box2, group2, own2, slots, sends, recvs
+):
+    me = [lax.axis_index(n) for n in ("gx", "gy", "gz")]
+    barrier = pltpu.get_barrier_semaphore()
+    for to in partners(me)[1]:
+        pl.semaphore_signal(barrier, inc=1, device_id=to, device_id_type=MESH)
+    group_inverse = inverse_of(top_state, 1)
+    total = None
+    for n, a in enumerate(leaves()):
+        x = product(group_inverse, far[a])
+        v[n] = x
+        g = gram_near_identity(x)
+        total = g if total is None else total + g
+    own2[...] = total
+    pl.semaphore_wait(barrier, 7)
+    copies = group_copies(me, own2, slots, sends, recvs)
+    for c in copies:
+        c.start()
     box_inverse = inverse_of(top_state, 0)
-    group_inverse = inverse_of(top_state, 1)
-    box_total = group_total = None
+    total = None
     for n, a in enumerate(leaves()):
-        rows = far[a]
-        x = product(inverse_of(leaf_state, n), rows)
-        q1[n] = x
-        grams2[n] = gram(x, stage)
-        x = product(box_inverse, rows)
-        w[n] = x
-        g = gram(x, stage)
-        box_total = g if box_total is None else box_total + g
-        x = product(group_inverse, rows)
-        v[n] = x
-        g = gram(x, stage)
-        group_total = g if group_total is None else group_total + g
-    box2[...] = box_total
-    group2[...] = group_total
+        both = jnp.concatenate([inverse_of(leaf_state, n), box_inverse], axis=0)
+        x = product(both, far[a])
+        q1[n] = x[:RANK]
+        w[n] = x[RANK:]
+        grams2[n] = gram_near_identity(x[:RANK])
+        g = gram_near_identity(x[RANK:])
+        total = g if total is None else total + g
+    box2[...] = total
+    collect(me, copies, own2, slots, group2)
 
 
 def second_kernel(q1, w, v, grams2, box2, group2, leaf_out, level_out, nested_out, leaf_state, top_state, stage):
@@ -384,23 +449,21 @@
         level_out[0, 0, 0, :, 2 * RANK * pair : 2 * RANK * (pair + 1)] = block
 
 
-def exchange_kernel(own, total, slots, sends, recvs):
-    names = ("gx", "gy", "gz")
-    me = [lax.axis_index(n) for n in names]
+def partners(me):
     bits = [m % 2 for m in me]
-    place = (bits[0] * 2 + bits[1]) * 2 + bits[2]
     others = []
     for n in range(1, 8):
         flip = (n // 4, n // 2 % 2, n % 2)
         others.append(tuple(me[k] + flip[k] * (1 - 2 * bits[k]) for k in range(3)))
-    barrier = pltpu.get_barrier_semaphore()
-    for to in others:
-        pl.semaphore_signal(barrier, inc=1, device_id=to, device_id_type=MESH)
-    pl.semaphore_wait(barrier, 7)
-    copies = [
+    return (bits[0] * 2 + bits[1]) * 2 + bits[2], others
+
+
+def group_copies(me, own, slots, sends, recvs):
+    here, others = partners(me)
+    return [
         pltpu.make_async_remote_copy(
             src_ref=own,
-            dst_ref=slots.at[place],
+            dst_ref=slots.at[here],
             send_sem=sends.at[n],
             recv_sem=recvs.at[n],
             device_id=to,
@@ -408,9 +471,10 @@
         )
         for n, to in enumerate(others)
     ]
-    for c in copies:
-        c.start()
-    slots[place] = own[...]
+
+
+def collect(me, copies, own, slots, total):
+    slots[partners(me)[0]] = own[...]
     for c in copies:
         c.wait_recv()
     value = slots[0]
@@ -422,21 +486,6 @@
 
 
 VMEM = pl.BlockSpec(memory_space=pltpu.VMEM)
-
-
-def group_sum(own, number):
-    return pl.pallas_call(
-        exchange_kernel,
-        out_shape=jax.ShapeDtypeStruct(own.shape, F32),
-        in_specs=[VMEM],
-        out_specs=VMEM,
-        scratch_shapes=[
-            pltpu.VMEM((8,) + own.shape, F32),
-            pltpu.SemaphoreType.DMA((7,)),
-            pltpu.SemaphoreType.DMA((7,)),
-        ],
-        compiler_params=pltpu.CompilerParams(collective_id=number, has_side_effects=True),
-    )(own)
 
 
 def local(kernel, outs, scratch, *args):
@@ -450,32 +499,32 @@
     )(*args)
 
 
-def finish(far, reduce_group):
+def finish(far, grams, box, group):
     width = far.shape[4]
     square, slab = (RANK, 2 * RANK), (8, RANK, width)
     stage, state = (2 * RANK, width), (8 * RANK, 2 * RANK)
-    grams, box = local(gram_kernel, [(8,) + square, square], [stage], far)
-    group = reduce_group(box, 1)
-    q1, w, v, grams2, box2, group2 = local(
-        first_kernel,
-        [slab, slab, slab, (8,) + square, square, square],
-        [state, state, stage],
-        far,
-        grams,
-        box,
-        group,
-    )
-    group2 = reduce_group(group2, 2)
+    states = local(first_kernel, [state, state], [], grams, box, group)
+    outs = [slab, slab, slab, (8,) + square, square, square]
+    applied = pl.pallas_call(
+        apply_kernel,
+        out_shape=[jax.ShapeDtypeStruct(s, F32) for s in outs],
+        in_specs=[VMEM] * 3,
+        out_specs=[VMEM] * 6,
+        scratch_shapes=[
+            pltpu.VMEM(square, F32),
+            pltpu.VMEM((8,) + square, F32),
+            pltpu.SemaphoreType.DMA((7,)),
+            pltpu.SemaphoreType.DMA((7,)),
+        ],
+        compiler_params=pltpu.CompilerParams(
+            collective_id=1, has_side_effects=True, vmem_limit_bytes=48 << 20
+        ),
+    )(far, *states)
     return local(
         second_kernel,
         [far.shape, (1, 1, 1, RANK, 8 * RANK), far.shape],
         [state, state, stage],
-        q1,
-        w,
-        v,
-        grams2,
-        box2,
-        group2,
+        *applied,
     )
 
 
@@ -488,8 +537,8 @@
     )
 
     def body(sketch, test_matrix, offsets, near):
-        far = near_field(mesh, sketch, test_matrix, offsets, near)
-        return tuple(finish(far, group_sum))
+        near_results = near_field(mesh, sketch, test_matrix, offsets, near)
+        return tuple(finish(*near_results))
 
     return jax.shard_map(
         body,

time: 113 us -> 87.3 us (0.77)
  Pallas kernels: 105 us -> 83.5 us
  local copies, waits for them, and re-layouts: 7.21 us -> 2.83 us
    pallas_call x3 -> x2, Pallas kernels: 33.2 us -> 20.2 us  [local(): pl.pallas_call(kernel, out_shape=[jax.ShapeDtypeStruct(s, F32) for s in o...]
    pallas_call x3 -> x2, Pallas kernels: 71.6 us -> 63.3 us  [the longest x1 55.3 us: near_field(): pl.pallas_call(functools.partial(near_kernel, sizes), out_shape=[jax.Shap...]
    unnamed x21 -> x7, local copies, waits for them, and re-layouts: 7.21 us -> 2.83 us
where the time goes in v2:
time: 87.3 us; the launch traced here: 87 us
  Pallas kernels  83.5 us (96%)
  local copies, waits for them, and re-layouts  2.83 us (3%)
    pallas_call x1, Pallas kernels, near_field(): pl.pallas_call(functools.partial(near_kernel, sizes), out_shape=[jax.Shap...  55.3 us
    pallas_call x2, Pallas kernels, local(): pl.pallas_call(kernel, out_shape=[jax.ShapeDtypeStruct(s, F32) for s in o...  20.2 us
    pallas_call x1, Pallas kernels, finish(): pl.pallas_call(apply_kernel, out_shape=[jax.ShapeDtypeStruct(s, F32) for...  7.98 us
    unnamed x7, local copies, waits for them, and re-layouts  2.83 us

profile of v2, /device:TPU:81, one launch (start us, length us, event | category | flops | bytes accessed | tf_op | source)
XLA Modules:
  0.0 87.0 jit_solution(3202209190588315321)
XLA Ops:
  0.6 0.0 copy-start.2
  0.6 0.7 copy.7.offs
  1.3 0.0 copy-done.2
  1.3 0.0 copy-start
  1.4 1.1 %copy-done = f32[2,2,2,64,384]{4,3,2,1,0:T(8,128)S(1)} copy-done((f32[2,2,2,64,384]{4,3,2,1,0:T(8,128)S(1)}, f32[2,2,2,64,384]{4,3,2,1,0:T(8,128)}, u32[]{:S(2)}) %copy-start) | copy-done | bytes 786456
  2.5 0.0 copy-start.1
  2.5 1.0 %copy-done.1 = bf16[2,2,2,64,384]{4,3,2,1,0:T(8,128)(2,1)S(1)} copy-done((bf16[2,2,2,64,384]{4,3,2,1,0:T(8,128)(2,1)S(1)}, bf16[2,2,2,64,384]{4,3,2,1,0:T(8,128)(2,1)}, u32[]{:S(2)}) %copy-start.1) | copy-done | bytes 393240
  3.5 55.3 %shard_map.67 = (f32[2,2,2,64,384]{4,3,2,1,0:T(8,128)S(1)}, f32[8,64,128]{2,1,0:T(8,128)S(1)}, f32[64,128]{1,0:T(8,128)S(1)}, f32[64,128]{1,0:T(8,128)S(1)}) custom-call(s32[2,2,2,27]{3,2,1,0:T(2,128)S(1)} %copy-done.2, f32[2,2,2,64,384]{4,3,2,1,0:T(8,128)S(1)} %copy-done, bf16[2,2,2,64,384]{4,3,2,1,0:T(8,128)(2,1)S(1)} %copy-done.1, ...), custom_call_target="tpu_custom_call" | custom-call | tf_op jit(solution)/shard_map/pallas_call | solution.py:265
  58.8 8.0 %shard_map.68 = (f32[512,128]{1,0:T(8,128)S(1)}, f32[512,128]{1,0:T(8,128)S(1)}) custom-call(f32[8,64,128]{2,1,0:T(8,128)S(1)} %get-tuple-element.16.grams, f32[64,128]{1,0:T(8,128)S(1)} %get-tuple-element.17.box, f32[64,128]{1,0:T(8,128)S(1)} %get-tuple-element.18.group), custom_call_target="tpu_custom_call" | custom-call | tf_op jit(solution)/shard_map/pallas_call | solution.py:492
  66.8 8.0 %shard_map.69 = (f32[8,64,384]{2,1,0:T(8,128)S(1)}, f32[8,64,384]{2,1,0:T(8,128)S(1)}, f32[8,64,384]{2,1,0:T(8,128)S(1)}, f32[8,64,128]{2,1,0:T(8,128)S(1)}, f32...) custom-call(f32[2,2,2,64,384]{4,3,2,1,0:T(8,128)S(1)} %get-tuple-element.15.far, f32[512,128]{1,0:T(8,128)S(1)} %get-tuple-element.19.leaf_state, ...), custom_call_target="tpu_custom_call" | custom-call | tf_op jit(solution)/shard_map/pallas_call | solution.py:508
  74.8 12.2 %shard_map.70 = (f32[2,2,2,64,384]{4,3,2,1,0:T(8,128)}, f32[1,1,1,64,512]{4,3,2,1,0:T(8,128)}, f32[2,2,2,64,384]{4,3,2,1,0:T(8,128)}) custom-call(f32[8,64,384]{2,1,0:T(8,128)S(1)} %get-tuple-element.21.q1, f32[8,64,384]{2,1,0:T(8,128)S(1)} %get-tuple-element.22.w, f32[8,64,384]{2,1,0:T(8,128)S(1)} %get-tuple-element.23.v, ...), custom_call_target="tpu_custom_call" | custom-call | tf_op jit(solution)/shard_map/pallas_call | solution.py:492
Async XLA Ops:
  0.6 0.7 copy-start.2
  1.3 1.1 %copy-start = (f32[2,2,2,64,384]{4,3,2,1,0:T(8,128)S(1)}, f32[2,2,2,64,384]{4,3,2,1,0:T(8,128)}, u32[]{:S(2)}) copy-start(f32[2,2,2,64,384]{4,3,2,1,0:T(8,128)} %sketch.1) | copy-start | bytes 2359300
  2.5 1.0 %copy-start.1 = (bf16[2,2,2,64,384]{4,3,2,1,0:T(8,128)(2,1)S(1)}, bf16[2,2,2,64,384]{4,3,2,1,0:T(8,128)(2,1)}, u32[]{:S(2)}) copy-start(bf16[2,2,2,64,384]{4,3,2,1,0:T(8,128)(2,1)} %test.1) | copy-start | bytes 1179652

commit v3 on v2

--- a/solution.py
+++ b/solution.py
@@ -165,6 +165,7 @@
     o_recvs,
     g_sends,
     g_recvs,
+    fetch_sem,
 ):
     names = ("gx", "gy", "gz")
     me = [lax.axis_index(n) for n in names]
@@ -200,6 +201,8 @@
             ),
         )
 
+    fetch = pltpu.make_async_copy(sketch, far, fetch_sem)
+    fetch.start()
     barrier = pltpu.get_barrier_semaphore()
     for d in directions():
 
@@ -234,7 +237,7 @@
     prepare(pick, rows8)
     ext[1:3, 1:3, 1:3] = test[...]
     ext_off[1:3, 1:3, 1:3] = offs[...]
-    far[...] = sketch[...]
+    fetch.wait()
 
     def arrive(kind, c):
         for d in order:
@@ -268,7 +271,12 @@
             jax.ShapeDtypeStruct(s, F32)
             for s in (sketch.shape, (8, RANK, 2 * RANK), (RANK, 2 * RANK), (RANK, 2 * RANK))
         ],
-        in_specs=[pl.BlockSpec(memory_space=pltpu.SMEM), vmem, vmem, vmem],
+        in_specs=[
+            pl.BlockSpec(memory_space=pltpu.SMEM),
+            pl.BlockSpec(memory_space=pl.ANY),
+            vmem,
+            vmem,
+        ],
         out_specs=[vmem] * 4,
         scratch_shapes=[
             pltpu.VMEM((4, 4, 4) + test.shape[3:], BF16),
@@ -285,6 +293,7 @@
             pltpu.SemaphoreType.DMA((26,)),
             pltpu.SemaphoreType.DMA((7,)),
             pltpu.SemaphoreType.DMA((7,)),
+            pltpu.SemaphoreType.DMA,
         ],
         compiler_params=pltpu.CompilerParams(
             collective_id=0, has_side_effects=True, vmem_limit_bytes=48 << 20
@@ -307,15 +316,30 @@
     return jnp.dot(left, right, precision=HIGHEST, preferred_element_type=F32)
 
 
-def gram_near_identity(rows):
-    high = rows.astype(BF16)
-    low = (rows - high.astype(F32)).astype(BF16)
-    both = jnp.concatenate([high, low], axis=0)
+def halves(x):
+    high = x.astype(BF16)
+    return high, (x - high.astype(F32)).astype(BF16)
+
+
+def rows_product(left, right):
+    left = jnp.concatenate(halves(left), axis=0)
+    right = jnp.concatenate(halves(right), axis=0)
     parts = lax.dot_general(
-        both, both, (((1,), (1,)), ((), ())), preferred_element_type=F32
+        left, right, (((1,), (1,)), ((), ())), preferred_element_type=F32
     )
     half = parts[:RANK] + parts[RANK:]
     return half + pltpu.roll(half, RANK, axis=1)
+
+
+def gram_near_identity(rows):
+    return rows_product(rows, rows)
+
+
+def near_product(left, right):
+    lefts, (high, low) = halves(left), halves(right)
+    parts = jnp.dot(jnp.concatenate(lefts, axis=0), high, preferred_element_type=F32)
+    rest = jnp.dot(lefts[0], low, preferred_element_type=F32)
+    return parts[:RANK] + (parts[RANK:] + rest)
 
 
 def with_eye(matrix):
@@ -324,42 +348,62 @@
     return jnp.where(lane < RANK, (row == lane).astype(F32), matrix)
 
 
-def put(state, slot, matrix):
-    state[pl.ds(slot, RANK, stride=8), :] = with_eye(matrix)
-
-
-def inverse_of(state, slot):
-    return state[pl.ds(slot, RANK, stride=8), :][:, :RANK]
+def put(state, slot, matrix, stride=8):
+    state[pl.ds(slot, RANK, stride=stride), :] = with_eye(matrix)
+
+
+def inverse_of(state, slot, stride=8):
+    return state[pl.ds(slot, RANK, stride=stride), :][:, :RANK]
 
 
 def splat(row, lane):
     return jnp.broadcast_to(row[:, RANK + lane : RANK + lane + 1], row.shape)
 
 
-def factor(states):
+def eliminate(rows, start):
+    c = {
+        (k, m): splat(rows[k], start + m) for k in range(BLOCK) for m in range(k, BLOCK)
+    }
+    for k in range(BLOCK):
+        inverse = lax.rsqrt(c[k, k])
+        f = {m: c[k, m] * inverse for m in range(k + 1, BLOCK)}
+        for m in range(k + 1, BLOCK):
+            for n in range(m, BLOCK):
+                c[m, n] = c[m, n] - f[m] * f[n]
+        rows[k] = rows[k] * inverse
+        for m in range(k + 1, BLOCK):
+            rows[m] = rows[m] - f[m] * rows[k]
+
+
+def factor(state, top):
+    sublane = lax.broadcasted_iota(jnp.int32, (8, 2 * RANK), 0)
     for start in range(0, RANK, BLOCK):
-        for state in states:
-            rows = [state[8 * (start + k) : 8 * (start + k) + 8, :] for k in range(BLOCK)]
-            c = {
-                (k, m): splat(rows[k], start + m)
-                for k in range(BLOCK)
-                for m in range(k, BLOCK)
-            }
+        rows = [state[8 * (start + k) : 8 * (start + k) + 8, :] for k in range(BLOCK)]
+        eliminate(rows, start)
+        for k in range(BLOCK):
+            state[8 * (start + k) : 8 * (start + k) + 8, :] = rows[k]
+        for i in range(start + BLOCK, RANK):
+            row = state[8 * i : 8 * i + 8, :]
             for k in range(BLOCK):
-                inverse = lax.rsqrt(c[k, k])
-                f = {m: c[k, m] * inverse for m in range(k + 1, BLOCK)}
-                for m in range(k + 1, BLOCK):
-                    for n in range(m, BLOCK):
-                        c[m, n] = c[m, n] - f[m] * f[n]
-                rows[k] = rows[k] * inverse
-                for m in range(k + 1, BLOCK):
-                    rows[m] = rows[m] - f[m] * rows[k]
-                state[8 * (start + k) : 8 * (start + k) + 8, :] = rows[k]
-            for i in range(start + BLOCK, RANK):
-                row = state[8 * i : 8 * i + 8, :]
-                for k in range(BLOCK):
-                    row = row - splat(rows[k], i) * rows[k]
-                state[8 * i : 8 * i + 8, :] = row
+                row = row - splat(rows[k], i) * rows[k]
+            state[8 * i : 8 * i + 8, :] = row
+        at = [slice(2 * (start + k), 2 * (start + k) + 2) for k in range(BLOCK)]
+        rows = [jnp.concatenate([top[at[k], :]] * 4, axis=0) for k in range(BLOCK)]
+        eliminate(rows, start)
+        turned = []
+        for k in range(BLOCK):
+            top[at[k], :] = rows[k][:2]
+            turn = rows[k]
+            for t in range(1, 4):
+                turn = jnp.where(
+                    sublane // 2 == t, pltpu.roll(rows[k], 2 * RANK - t, axis=1), turn
+                )
+            turned.append(turn)
+        for i in range(start + BLOCK, RANK, 4):
+            four = top[2 * i : 2 * i + 8, :]
+            for k in range(BLOCK):
+                four = four - splat(turned[k], i) * rows[k]
+            top[2 * i : 2 * i + 8, :] = four
 
 
 def leaves():
@@ -379,10 +423,9 @@
 def first_kernel(grams, box, group, leaf_state, top_state):
     for n in range(8):
         put(leaf_state, n, grams[n])
-    put(top_state, 0, box[...])
-    for n in range(1, 8):
-        put(top_state, n, group[...])
-    factor([leaf_state, top_state])
+    put(top_state, 0, box[...], 2)
+    put(top_state, 1, group[...], 2)
+    factor(leaf_state, top_state)
 
 
 def apply_kernel(
@@ -392,7 +435,7 @@
     barrier = pltpu.get_barrier_semaphore()
     for to in partners(me)[1]:
         pl.semaphore_signal(barrier, inc=1, device_id=to, device_id_type=MESH)
-    group_inverse = inverse_of(top_state, 1)
+    group_inverse = inverse_of(top_state, 1, 2)
     total = None
     for n, a in enumerate(leaves()):
         x = product(group_inverse, far[a])
@@ -404,7 +447,7 @@
     copies = group_copies(me, own2, slots, sends, recvs)
     for c in copies:
         c.start()
-    box_inverse = inverse_of(top_state, 0)
+    box_inverse = inverse_of(top_state, 0, 2)
     total = None
     for n, a in enumerate(leaves()):
         both = jnp.concatenate([inverse_of(leaf_state, n), box_inverse], axis=0)
@@ -418,35 +461,27 @@
     collect(me, copies, own2, slots, group2)
 
 
-def second_kernel(q1, w, v, grams2, box2, group2, leaf_out, level_out, nested_out, leaf_state, top_state, stage):
+def second_kernel(q1, w, v, grams2, box2, group2, leaf_out, level_out, nested_out, leaf_state, top_state):
     for n in range(8):
         put(leaf_state, n, grams2[n])
-    put(top_state, 0, box2[...])
-    for n in range(1, 8):
-        put(top_state, n, group2[...])
-    factor([leaf_state, top_state])
+    put(top_state, 0, box2[...], 2)
+    put(top_state, 1, group2[...], 2)
+    factor(leaf_state, top_state)
     width = q1.shape[2]
-    box_inverse = inverse_of(top_state, 0) * math.sqrt(8 * RANK)
-    group_inverse = inverse_of(top_state, 1) * (8.0 * math.sqrt(width))
+    box_inverse = inverse_of(top_state, 0, 2) * math.sqrt(8 * RANK)
+    group_inverse = inverse_of(top_state, 1, 2) * (8.0 * math.sqrt(width))
+    left_lanes = lax.broadcasted_iota(jnp.int32, (RANK, 2 * RANK), 1) < RANK
     for pair in range(4):
-        block = None
-        for half in range(2):
-            n = 2 * pair + half
+        blocks = []
+        for n in (2 * pair, 2 * pair + 1):
             a = leaves()[n]
-            x = product(inverse_of(leaf_state, n), q1[n])
+            x = near_product(inverse_of(leaf_state, n), q1[n])
             leaf_out[a] = x * math.sqrt(width)
-            nested_out[a] = product(group_inverse, v[n])
-            stage[half * RANK : (half + 1) * RANK, :] = x
-            stage[(1 - half) * RANK : (2 - half) * RANK, :] = jnp.zeros((RANK, width), F32)
-            part = lax.dot_general(
-                product(box_inverse, w[n]),
-                stage[...],
-                (((1,), (1,)), ((), ())),
-                precision=HIGHEST,
-                preferred_element_type=F32,
-            )
-            block = part if block is None else block + part
-        level_out[0, 0, 0, :, 2 * RANK * pair : 2 * RANK * (pair + 1)] = block
+            nested_out[a] = near_product(group_inverse, v[n])
+            blocks.append(rows_product(near_product(box_inverse, w[n]), x))
+        level_out[0, 0, 0, :, 2 * RANK * pair : 2 * RANK * (pair + 1)] = jnp.where(
+            left_lanes, blocks[0], blocks[1]
+        )
 
 
 def partners(me):
@@ -502,8 +537,8 @@
 def finish(far, grams, box, group):
     width = far.shape[4]
     square, slab = (RANK, 2 * RANK), (8, RANK, width)
-    stage, state = (2 * RANK, width), (8 * RANK, 2 * RANK)
-    states = local(first_kernel, [state, state], [], grams, box, group)
+    state = (8 * RANK, 2 * RANK)
+    states = local(first_kernel, [state, (2 * RANK, 2 * RANK)], [], grams, box, group)
     outs = [slab, slab, slab, (8,) + square, square, square]
     applied = pl.pallas_call(
         apply_kernel,
@@ -523,7 +558,7 @@
     return local(
         second_kernel,
         [far.shape, (1, 1, 1, RANK, 8 * RANK), far.shape],
-        [state, state, stage],
+        [state, (2 * RANK, 2 * RANK)],
         *applied,
     )
 

time: 87.3 us -> 83 us (0.951)
  Pallas kernels: 83.5 us -> 79.3 us
    pallas_call x2, Pallas kernels: 20.2 us -> 15.9 us  [local(): pl.pallas_call(kernel, out_shape=[jax.ShapeDtypeStruct(s, F32) for s in o...]
where the time goes in v3:
time: 83 us; the launch traced here: 82.8 us
  Pallas kernels  79.3 us (96%)
  local copies, waits for them, and re-layouts  2.83 us (3%)
    pallas_call x1, Pallas kernels, near_field(): pl.pallas_call(functools.partial(near_kernel, sizes), out_shape=[jax.Shap...  55.4 us
    pallas_call x2, Pallas kernels, local(): pl.pallas_call(kernel, out_shape=[jax.ShapeDtypeStruct(s, F32) for s in o...  15.9 us
    pallas_call x1, Pallas kernels, finish(): pl.pallas_call(apply_kernel, out_shape=[jax.ShapeDtypeStruct(s, F32) for...  7.98 us
    unnamed x7, local copies, waits for them, and re-layouts  2.83 us

profile of v3, /device:TPU:81, one launch (start us, length us, event | category | flops | bytes accessed | tf_op | source)
XLA Modules:
  0.0 82.8 jit_solution(7129569215683229717)
XLA Ops:
  0.6 0.0 copy-start.2
  0.6 0.7 copy.7.offs
  1.3 0.0 copy-done.2
  1.3 0.0 copy-start
  1.4 1.1 %copy-done = f32[2,2,2,64,384]{4,3,2,1,0:T(8,128)S(1)} copy-done((f32[2,2,2,64,384]{4,3,2,1,0:T(8,128)S(1)}, f32[2,2,2,64,384]{4,3,2,1,0:T(8,128)}, u32[]{:S(2)}) %copy-start) | copy-done | bytes 786456
  2.5 0.0 copy-start.1
  2.5 1.0 %copy-done.1 = bf16[2,2,2,64,384]{4,3,2,1,0:T(8,128)(2,1)S(1)} copy-done((bf16[2,2,2,64,384]{4,3,2,1,0:T(8,128)(2,1)S(1)}, bf16[2,2,2,64,384]{4,3,2,1,0:T(8,128)(2,1)}, u32[]{:S(2)}) %copy-start.1) | copy-done | bytes 393240
  3.5 55.4 %shard_map.67 = (f32[2,2,2,64,384]{4,3,2,1,0:T(8,128)S(1)}, f32[8,64,128]{2,1,0:T(8,128)S(1)}, f32[64,128]{1,0:T(8,128)S(1)}, f32[64,128]{1,0:T(8,128)S(1)}) custom-call(s32[2,2,2,27]{3,2,1,0:T(2,128)S(1)} %copy-done.2, f32[2,2,2,64,384]{4,3,2,1,0:T(8,128)S(1)} %copy-done, bf16[2,2,2,64,384]{4,3,2,1,0:T(8,128)(2,1)S(1)} %copy-done.1, ...), custom_call_target="tpu_custom_call" | custom-call | tf_op jit(solution)/shard_map/pallas_call | solution.py:268
  58.9 6.3 %shard_map.68 = (f32[512,128]{1,0:T(8,128)S(1)}, f32[128,128]{1,0:T(8,128)S(1)}) custom-call(f32[8,64,128]{2,1,0:T(8,128)S(1)} %get-tuple-element.16.grams, f32[64,128]{1,0:T(8,128)S(1)} %get-tuple-element.17.box, f32[64,128]{1,0:T(8,128)S(1)} %get-tuple-element.18.group), custom_call_target="tpu_custom_call" | custom-call | tf_op jit(solution)/shard_map/pallas_call | solution.py:527
  65.2 8.0 %shard_map.69 = (f32[8,64,384]{2,1,0:T(8,128)S(1)}, f32[8,64,384]{2,1,0:T(8,128)S(1)}, f32[8,64,384]{2,1,0:T(8,128)S(1)}, f32[8,64,128]{2,1,0:T(8,128)S(1)}, f32...) custom-call(f32[2,2,2,64,384]{4,3,2,1,0:T(8,128)S(1)} %get-tuple-element.15.far, f32[512,128]{1,0:T(8,128)S(1)} %get-tuple-element.19.leaf_state, ...), custom_call_target="tpu_custom_call" | custom-call | tf_op jit(solution)/shard_map/pallas_call | solution.py:543
  73.2 9.5 %shard_map.70 = (f32[2,2,2,64,384]{4,3,2,1,0:T(8,128)}, f32[1,1,1,64,512]{4,3,2,1,0:T(8,128)}, f32[2,2,2,64,384]{4,3,2,1,0:T(8,128)}) custom-call(f32[8,64,384]{2,1,0:T(8,128)S(1)} %get-tuple-element.21.q1, f32[8,64,384]{2,1,0:T(8,128)S(1)} %get-tuple-element.22.w, f32[8,64,384]{2,1,0:T(8,128)S(1)} %get-tuple-element.23.v, ...), custom_call_target="tpu_custom_call" | custom-call | tf_op jit(solution)/shard_map/pallas_call | solution.py:527
Async XLA Ops:
  0.6 0.7 copy-start.2
  1.3 1.1 %copy-start = (f32[2,2,2,64,384]{4,3,2,1,0:T(8,128)S(1)}, f32[2,2,2,64,384]{4,3,2,1,0:T(8,128)}, u32[]{:S(2)}) copy-start(f32[2,2,2,64,384]{4,3,2,1,0:T(8,128)} %sketch.1) | copy-start | bytes 2359300
  2.5 1.0 %copy-start.1 = (bf16[2,2,2,64,384]{4,3,2,1,0:T(8,128)(2,1)S(1)}, bf16[2,2,2,64,384]{4,3,2,1,0:T(8,128)(2,1)}, u32[]{:S(2)}) copy-start(bf16[2,2,2,64,384]{4,3,2,1,0:T(8,128)(2,1)} %test.1) | copy-start | bytes 1179652
